TPU v7x, 32 devices: a whole 2x2x4 slice. The times are simulated.
32 devices in a mesh: samp: 8 (over z, y), feat: 4 (over x, core).
Axes of the slice: x: 2, y: 2, z: 4, core: 2. Of those that a mesh axis runs over, the one named last changes fastest.
Arguments:
- data: bfloat16 [8192, 4096], P('samp', 'feat'), may hold values from -0.09375 to 0.09375
- targets: float32 [8192, 256], P('samp'), may hold values from -24 to 24
- tile_x: float32 [8, 4096, 256], P('samp', 'feat'), may hold values from -6 to 6
- x_dual: float32 [8, 4096, 256], P('samp', 'feat'), may hold values from -6 to 6
- tile_y: float32 [4, 8192, 256], P('feat', 'samp'), may hold values from -6 to 6
- y_dual: float32 [4, 8192, 256], P('feat', 'samp'), may hold values from -6 to 6
Outputs:
- new_x: float32 [8, 4096, 256], P('samp', 'feat')
- new_x_dual: float32 [8, 4096, 256], P('samp', 'feat')
- new_y: float32 [4, 8192, 256], P('feat', 'samp')
- new_y_dual: float32 [4, 8192, 256], P('feat', 'samp')
All inputs are finite; a program needn't handle non-finite values.
Results may differ from a plain program's by a relative error of at most 0.0041.
Values sent between devices are 32-bit elements; how exact they have to be, the bound alone decides.
A program may use at most 128 MiB of HBM per device.

v0:
```python
import jax
import jax.numpy as jnp
from jax import lax
from jax.sharding import PartitionSpec as P

ITERS = 2
huber_width = 0.5
shrink_level = 0.1
f32 = jnp.float32
bf16 = jnp.bfloat16


def soft_shrink(values):
    return jnp.sign(values) * jnp.maximum(jnp.abs(values) - shrink_level, 0.0)


def huber_prox(values, weight):
    limit = huber_width * (1.0 + weight)
    return jnp.where(
        jnp.abs(values) <= limit,
        values / (1.0 + weight),
        values - weight * huber_width * jnp.sign(values),
    )


def dot(a, b):
    return jnp.dot(a, b, preferred_element_type=f32)


def shards(data, targets, tile_x, x_dual, tile_y, y_dual):
    n_samp = lax.axis_size("samp")
    n_feat = lax.axis_size("feat")
    order = data.shape[0]
    q = tile_x[0] + x_dual[0]
    p = tile_y[0] + y_dual[0]
    gram = lax.dot_general(data, data, (((1,), (1,)), ((), ())), preferred_element_type=f32)
    identity = jnp.eye(order, dtype=f32)
    wide = data.astype(f32)
    factor = 1.0 / (1.0 + 2.0 * jnp.sum(wide * wide) / order)
    a = 2.0 * factor - factor * factor
    b = factor * factor
    g16 = gram.astype(bf16)
    inner = (2.0 - a) * identity + (b - a) * gram + b * dot(g16, g16)
    inverse = a * inner - b * dot(g16, inner.astype(bf16))
    back_map = lax.dot_general(
        data, inverse.astype(bf16), (((0,), (0,)), ((), ())), preferred_element_type=f32
    ).astype(bf16)
    for turn_index in range(ITERS):
        consensus = soft_shrink(lax.psum(q, "samp") / n_samp)
        total = lax.psum(p, "feat")
        correction = (targets + huber_prox(total - targets, float(n_feat)) - total) / n_feat
        dual = q - consensus
        start = consensus - dual
        aim = p + 2.0 * correction
        ahead = dot(data, start.astype(bf16))
        back = dot(back_map, (ahead - aim).astype(bf16))
        coeffs = start - back
        partials = ahead - dot(data, back.astype(bf16))
        q = consensus - back
        p = partials - correction
    return (coeffs[None], dual[None], partials[None], -correction[None])


def solution(mesh):
    return jax.shard_map(
        shards,
        mesh=mesh,
        in_specs=(
            P("samp", "feat"),
            P("samp", None),
            P("samp", "feat", None),
            P("samp", "feat", None),
            P("feat", "samp", None),
            P("feat", "samp", None),
        ),
        out_specs=(
            P("samp", "feat", None),
            P("samp", "feat", None),
            P("feat", "samp", None),
            P("feat", "samp", None),
        ),
        check_vma=False,
    )
```

profile of v0, /device:TPU:0, one launch (start us, length us, event | category | flops | bytes accessed | tf_op | source)
XLA Modules:
  0.0 277.3 jit_solution(14655936725483755482)
XLA Ops:
  7.2 0.0 copy-start.10
  7.2 0.0 all-reduce.5.cloned.1.call-start
  7.2 2.7 add_bitcast_fusion.1
  9.9 0.0 copy-start.11
  9.9 0.0 all-reduce.5.cloned.1.call-update
  10.0 0.0 all-reduce.7.cloned.1.call-start
  10.0 0.0 copy-done.10
  10.0 0.3 copy.10
  10.4 0.8 copy-done.11
  11.2 1.3 copy.11
  12.5 0.0 copy-start
  12.5 2.5 add_bitcast_fusion
  15.0 0.0 all-reduce.7.cloned.1.call-update
  15.0 0.0 all-reduce.11.cloned.1.call-start
  15.0 0.0 copy-done
  15.0 1.7 multiply_reduce_fusion
  17.4 2.4 fusion.34
  19.8 0.0 copy-start.12
  19.8 2.0 copy-done.12
  21.8 4.3 %multiply_add_fusion = f32[1024,1024]{1,0:T(8,128)} fusion(f32[1024,1024]{1,0:T(8,128)S(1)} %fusion.34, f32[]{:T(128)S(6)} %mul.62, f32[]{:T(128)S(6)} %sub.72, f32[]{:T(128)S(6)} %sub.71), kind=kOutput, calls=%fused_computation.1 | convolution fusion | flops 2154823680 | bytes 8388620 | tf_op jit(solution)/shard_map/dot_general | solution.py:27
  26.1 10.7 %convolution_convert_fusion = bf16[1024,1024]{1,0:T(8,128)(2,1)} fusion(bf16[1024,1024]{1,0:T(8,128)(2,1)S(1)} %copy-done, f32[1024,1024]{1,0:T(8,128)} %multiply_add_fusion, f32[]{:T(128)S(6)} %mul.62, f32[]{:T(128)S(6)} %sub.70, f32[1024,1024]{1,0:T(8,128)} %copy-done.12), kind=kOutput, calls=%fused_computation.5 | convolution fusion | flops 4302307328 | bytes 12582920 | tf_op jit(solution)/shard_map/dot_general | solution.py:45
  36.8 1.6 copy.13
  38.3 54.8 %all-reduce.5.cloned.1.call-done = f32[1024,256]{1,0:T(8,128)} async-done(((f32[1024,256]{1,0:T(8,128)}), f32[1024,256]{1,0:T(8,128)}) %all-reduce.5.cloned.1.call-update) | async-done | bytes 1048592 | tf_op jit(solution)/shard_map/psum | solution.py:49
  93.2 3.7 %convolution_bitcast_fusion.3 = f32[1024,256]{0,1:T(8,128)} fusion(bf16[1024,1024]{1,0:T(8,128)(2,1)S(1)} %copy-done, f32[1024,256]{1,0:T(8,128)} %add_bitcast_fusion.1, f32[1024,256]{1,0:T(8,128)} %all-reduce.5.cloned.1.call-done), kind=kOutput, calls=%fused_computation.10 | convolution fusion | flops 539230208 | bytes 5242880 | tf_op jit(solution)/shard_map/dot_general | solution.py:27
  96.8 35.2 %all-reduce.7.cloned.1.call-done = f32[1024,256]{0,1:T(8,128)} async-done(((f32[1024,256]{0,1:T(8,128)}), f32[1024,256]{0,1:T(8,128)}) %all-reduce.7.cloned.1.call-update) | async-done | bytes 1048592 | tf_op jit(solution)/shard_map/psum | solution.py:50
  132.0 0.0 copy-start.5
  132.0 0.0 copy-start.9
  132.0 5.3 %fusion.14 = (f32[1024,256]{1,0:T(8,128)}, bf16[1024,256]{1,0:T(8,128)(2,1)S(1)}) fusion(f32[1024,256]{1,0:T(8,128)} %all-reduce.5.cloned.1.call-done, bf16[1024,1024]{1,0:T(8,128)(2,1)} %convolution_convert_fusion, f32[1024,256]{0,1:T(8,128)} %convolution_bitcast_fusion.3, f32[1024,256]{0,1:T(8,128)} %add_bitcast_fusion, ...), kind=kOutput, calls=%fused_computation.34 | convolution fusion | flops 542638080 | bytes 8912896 | tf_op jit(solution)/shard_map/dot_general | solution.py:27
  137.3 0.0 copy-done.5
  137.3 0.0 copy-done.9
  137.3 2.4 fusion.2
  139.8 0.0 all-reduce.11.cloned.1.call-update
  139.8 0.0 all-reduce.9.cloned.1.call-start
  139.8 0.5 all-reduce.9.cloned.1.call-update
  140.4 36.4 %all-reduce.11.cloned.1.call-done = f32[1024,256]{0,1:T(8,128)} async-done(((f32[1024,256]{0,1:T(8,128)}), f32[1024,256]{0,1:T(8,128)}) %all-reduce.11.cloned.1.call-update) | async-done | bytes 1048592 | tf_op jit(solution)/shard_map/psum | solution.py:50
  176.7 2.8 %negate_bitcast_fusion = f32[1,1024,256]{1,2,0:T(8,128)} fusion(f32[1024,256]{0,1:T(8,128)} %all-reduce.11.cloned.1.call-done, f32[1024,256]{0,1:T(8,128)S(1)} %copy.13), kind=kLoop, calls=%fused_computation.16 | loop fusion | flops 3145728 | bytes 3145728 | tf_op jit(solution)/shard_map/neg | solution.py:61
  179.5 2.5 copy.17
  182.0 77.4 %all-reduce.9.cloned.1.call-done = f32[1024,256]{1,0:T(8,128)} async-done(((f32[1024,256]{1,0:T(8,128)}), f32[1024,256]{1,0:T(8,128)}) %all-reduce.9.cloned.1.call-update) | async-done | bytes 1048592 | tf_op jit(solution)/shard_map/psum | solution.py:49
  259.5 0.0 copy-start.2
  259.5 0.0 copy-start.6
  259.5 0.0 copy-start.7
  259.5 2.8 %convolution_bitcast_fusion.2 = f32[1024,256]{0,1:T(8,128)S(1)} fusion(bf16[1024,1024]{1,0:T(8,128)(2,1)S(1)} %copy-done, f32[1024,256]{1,0:T(8,128)} %get-tuple-element.10, f32[1024,256]{1,0:T(8,128)} %all-reduce.9.cloned.1.call-done), kind=kOutput, calls=%fused_computation.9 | convolution fusion | flops 539230208 | bytes 5242880 | tf_op jit(solution)/shard_map/dot_general | solution.py:27
  262.3 0.0 copy-done.2
  262.3 0.0 copy-done.6
  262.3 0.0 copy-done.7
  262.3 1.2 fusion.16
  263.5 0.0 copy-start.3
  263.5 1.0 copy-done.3
  264.5 0.0 copy-start.8
  264.5 1.8 fusion.4
  266.3 0.0 copy-start.1
  266.3 0.0 copy-start.4
  266.3 2.7 copy.16
  269.0 0.0 copy-done.8
  269.0 0.0 copy-done.1
  269.0 0.0 copy-done.4
  269.0 1.8 subtract_bitcast_fusion.1
Async XLA Ops:
  7.2 2.9 %copy-start.10 = (f32[1,1024,256]{2,1,0:T(8,128)S(1)}, f32[1,1024,256]{2,1,0:T(8,128)}, u32[]{:S(2)}) copy-start(f32[1,1024,256]{2,1,0:T(8,128)} %param.10) | copy-start | bytes 3145732
  7.2 86.0 %all-reduce.5.cloned.1.call-start = ((), (), s32[]{:S(2)}) async-start(), calls=%async_computation | async-start | bytes 2097152 | tf_op jit(solution)/shard_map/psum | solution.py:49
  9.9 1.2 copy-start.11
  10.0 122.1 %all-reduce.7.cloned.1.call-start = ((), (), s32[]{:S(2)}) async-start(), calls=%async_computation.1 | async-start | bytes 2097152 | tf_op jit(solution)/shard_map/psum | solution.py:50
  12.5 2.6 copy-start
  15.0 161.7 %all-reduce.11.cloned.1.call-start = ((), (), s32[]{:S(2)}) async-start(), calls=%async_computation.3 | async-start | bytes 2097152 | tf_op jit(solution)/shard_map/psum | solution.py:50
  19.8 2.0 copy-start.12
  132.0 5.3 %copy-start.5 = (f32[1024,256]{0,1:T(8,128)S(1)}, f32[1024,256]{0,1:T(8,128)}, u32[]{:S(2)}) copy-start(f32[1024,256]{0,1:T(8,128)} %convolution_bitcast_fusion.3) | copy-start | bytes 3145732
  132.0 5.3 %copy-start.9 = (f32[1024,256]{0,1:T(8,128)S(1)}, f32[1024,256]{0,1:T(8,128)}, u32[]{:S(2)}) copy-start(f32[1024,256]{0,1:T(8,128)} %all-reduce.7.cloned.1.call-done) | copy-start | bytes 3145732
  139.8 119.7 %all-reduce.9.cloned.1.call-start = ((), (), s32[]{:S(2)}) async-start(), calls=%async_computation.2 | async-start | bytes 2097152 | tf_op jit(solution)/shard_map/psum | solution.py:49
  259.5 2.9 %copy-start.2 = (bf16[1024,1024]{1,0:T(8,128)(2,1)S(1)}, bf16[1024,1024]{1,0:T(8,128)(2,1)}, u32[]{:S(2)}) copy-start(bf16[1024,1024]{1,0:T(8,128)(2,1)} %convolution_convert_fusion) | copy-start | bytes 6291460
  259.5 2.9 %copy-start.6 = (f32[1024,256]{0,1:T(8,128)S(1)}, f32[1024,256]{0,1:T(8,128)}, u32[]{:S(2)}) copy-start(f32[1024,256]{0,1:T(8,128)} %fusion.2) | copy-start | bytes 3145732
  259.5 2.9 %copy-start.7 = (f32[1024,256]{0,1:T(8,128)S(1)}, f32[1024,256]{0,1:T(8,128)}, u32[]{:S(2)}) copy-start(f32[1024,256]{0,1:T(8,128)} %all-reduce.11.cloned.1.call-done) | copy-start | bytes 3145732
  263.5 1.0 copy-start.3
  264.5 4.5 %copy-start.8 = (f32[1024,256]{1,0:T(8,128)S(1)}, f32[1024,256]{1,0:T(8,128)}, u32[]{:S(2)}) copy-start(f32[1024,256]{1,0:T(8,128)} %all-reduce.9.cloned.1.call-done) | copy-start | bytes 3145732
  266.3 2.7 copy-start.1
  266.3 2.7 copy-start.4
Sparse Core Ops, SparseCore 0:
  12.1 81.0 all-reduce.4
  96.1 35.8 all-reduce.6
  139.9 36.7 all-reduce.10
  180.7 78.7 all-reduce.8
where the time goes:
time: 278 us; the launch traced here: 277 us
  waiting for transfers between devices  204 us (73%)
  matrix products  34.6 us (12%)
  between operations  14.6 us (5%)
  local copies, waits for them, and re-layouts  12.2 us (4%)
  other arithmetic  11.5 us (4%)
    psum x2, waiting for transfers between devices, shards(): consensus = soft_shrink(lax.psum(q, 'samp') / n_samp)  132 us
    psum x2, waiting for transfers between devices, shards(): total = lax.psum(p, 'feat')  71.6 us
    dot_general x7, matrix products, dot(): return jnp.dot(a, b, preferred_element_type=f32)  21.5 us
    unnamed x31, local copies, waits for them, and re-layouts  12.2 us
    dot_general x1, matrix products, shards(): lax.dot_general(data, inverse.astype(bf16), (((0,), (0,)), ((), ())), pre...  10.7 us
  transfers between devices with their start and end apart: 4, of which 4 were waited for; matrix products, arithmetic and copies ran while one was open for 12% of the time, Pallas kernels for 0%

commit v1 on v0

--- a/solution.py
+++ b/solution.py
@@ -47,7 +47,7 @@
     ).astype(bf16)
     for turn_index in range(ITERS):
         consensus = soft_shrink(lax.psum(q, "samp") / n_samp)
-        total = lax.psum(p, "feat")
+        total = jnp.sum(lax.all_gather(p, "feat"), axis=0)
         correction = (targets + huber_prox(total - targets, float(n_feat)) - total) / n_feat
         dual = q - consensus
         start = consensus - dual

time: 278 us -> 226 us (0.81)
  waiting for transfers between devices: 204 us -> 130 us
  local copies, waits for them, and re-layouts: 12.2 us -> 22 us
  other arithmetic: 11.5 us -> 18.6 us
  matrix products: 34.6 us -> 38.5 us
    psum x2 -> x0, waiting for transfers between devices: 71.6 us -> none  [shards(): total = lax.psum(p, 'feat')]
    reduce_sum x0 -> x2, other arithmetic: none -> 9.27 us  [shards(): total = jnp.sum(lax.all_gather(p, 'feat'), axis=0)]
    all_gather x0 -> x1, local copies, waits for them, and re-layouts: none -> 6.06 us  [shards(): total = jnp.sum(lax.all_gather(p, 'feat'), axis=0)]
    dot_general x7, matrix products: 21.5 us -> 25.4 us  [dot(): return jnp.dot(a, b, preferred_element_type=f32)]
    unnamed x31 -> x27, local copies, waits for them, and re-layouts: 12.2 us -> 12.1 us
  transfers between devices with their start and end apart: 4 -> 4, of which waited for: 4 -> 2; matrix products, arithmetic and copies ran while one was open for 12% -> 15% of each run, Pallas kernels for 0% -> 0%
where the time goes in v1:
time: 226 us
  waiting for transfers between devices  130 us (58%)
  matrix products  38.5 us (17%)
  local copies, waits for them, and re-layouts  22 us (10%)
  other arithmetic  18.6 us (8%)
  between operations  16.3 us (7%)
    psum x2, waiting for transfers between devices, shards(): consensus = soft_shrink(lax.psum(q, 'samp') / n_samp)  130 us
    dot_general x7, matrix products, dot(): return jnp.dot(a, b, preferred_element_type=f32)  25.4 us
    unnamed x27, local copies, waits for them, and re-layouts  12.1 us
    dot_general x1, matrix products, shards(): lax.dot_general(data, inverse.astype(bf16), (((0,), (0,)), ((), ())), pre...  10.7 us
    reduce_sum x2, other arithmetic, shards(): total = jnp.sum(lax.all_gather(p, 'feat'), axis=0)  9.27 us
    all_gather x1, local copies, waits for them, and re-layouts, shards(): total = jnp.sum(lax.all_gather(p, 'feat'), axis=0)  6.06 us
  transfers between devices with their start and end apart: 4, of which 2 were waited for; matrix products, arithmetic and copies ran while one was open for 15% of the time, Pallas kernels for 0%

profile of v1, /device:TPU:0, one launch (start us, length us, event | category | flops | bytes accessed | tf_op | source)
XLA Modules:
  0.0 225.5 jit_solution(8071781964003973142)
XLA Ops:
  8.0 0.0 copy-start.8
  8.0 0.0 all-reduce.3.cloned.1.call-start
  8.1 2.7 %add_bitcast_fusion = f32[1024,256]{1,0:T(8,128)} fusion(f32[1,1024,256]{2,1,0:T(8,128)} %param.8, f32[1,1024,256]{2,1,0:T(8,128)} %param.9), kind=kLoop, calls=%fused_computation.32 | loop fusion | flops 262144 | bytes 3145728 | tf_op jit(solution)/shard_map/add | solution.py:34
  10.8 0.0 copy-start.9
  10.8 0.0 all-reduce.3.cloned.1.call-update
  10.8 0.0 all-gather.4.cloned.1.call-start
  10.9 0.0 copy-done.8
  10.9 0.3 copy.27
  11.2 0.8 copy-done.9
  12.0 0.3 copy.28
  12.3 0.1 add.45
  12.5 0.0 copy-start.6
  12.5 0.0 copy-start
  12.5 1.3 copy.29
  13.8 0.0 all-gather.4.cloned.1.call-update
  13.8 0.0 all-reduce.5.cloned.1.call-start
  13.9 1.0 copy-done
  14.8 1.7 multiply_reduce_fusion
  16.5 0.0 copy-done.6
  17.2 1.6 copy.32
  18.8 2.4 %fusion.37 = f32[1024,1024]{1,0:T(8,128)S(1)} fusion(bf16[1024,1024]{1,0:T(8,128)(2,1)S(1)} %copy-done), kind=kOutput, calls=%fused_computation.54 | convolution fusion | flops 2147483648 | bytes 6291456 | tf_op jit(solution)/shard_map/dot_general | solution.py:36
  21.2 0.0 copy-start.10
  21.2 2.0 copy-done.10
  23.1 4.3 %multiply_add_fusion = f32[1024,1024]{1,0:T(8,128)} fusion(f32[1024,1024]{1,0:T(8,128)S(1)} %fusion.37, f32[]{:T(128)S(6)} %mul.62, f32[]{:T(128)S(6)} %sub.72, f32[]{:T(128)S(6)} %sub.71), kind=kOutput, calls=%fused_computation.1 | convolution fusion | flops 2154823680 | bytes 8388620 | tf_op jit(solution)/shard_map/dot_general | solution.py:27
  27.5 10.7 %convolution_convert_fusion = bf16[1024,1024]{1,0:T(8,128)(2,1)} fusion(bf16[1024,1024]{1,0:T(8,128)(2,1)S(1)} %copy-done, f32[1024,1024]{1,0:T(8,128)} %multiply_add_fusion, f32[]{:T(128)S(6)} %mul.62, f32[]{:T(128)S(6)} %sub.70, f32[1024,1024]{1,0:T(8,128)} %copy-done.10), kind=kOutput, calls=%fused_computation.5 | convolution fusion | flops 4302307328 | bytes 12582920 | tf_op jit(solution)/shard_map/dot_general | solution.py:45
  38.2 55.8 %all-reduce.3.cloned.1.call-done = f32[1024,256]{1,0:T(8,128)} async-done(((f32[1024,256]{1,0:T(8,128)}), f32[1024,256]{1,0:T(8,128)}) %all-reduce.3.cloned.1.call-update) | async-done | bytes 1048592 | tf_op jit(solution)/shard_map/psum | solution.py:49
  94.0 3.7 %convolution_bitcast_fusion.3 = f32[1024,256]{0,1:T(8,128)} fusion(bf16[1024,1024]{1,0:T(8,128)(2,1)S(1)} %copy-done, f32[1024,256]{1,0:T(8,128)} %add_bitcast_fusion, f32[1024,256]{1,0:T(8,128)} %all-reduce.3.cloned.1.call-done), kind=kOutput, calls=%fused_computation.10 | convolution fusion | flops 539230208 | bytes 5242880 | tf_op jit(solution)/shard_map/dot_general | solution.py:27
  97.6 0.0 all-gather.4.cloned.1.call-done
  97.6 3.6 %reduce_sum.28 = f32[1024,256]{1,0:T(8,128)} reduce(f32[4,1024,256]{2,1,0:T(8,128)} %all-gather.4.cloned.1.call-done, f32[]{:T(128)} %constant.26.clone.1), dimensions={0}, to_apply=%region_2.0 | reduce | flops 786432 | bytes 5242884 | tf_op jit(solution)/shard_map/reduce_sum | solution.py:50
  101.2 2.5 %copy.30 = f32[1024,256]{0,1:T(8,128)} copy(f32[1024,256]{1,0:T(8,128)} %reduce_sum.28) | data formatting | bytes 2097152 | tf_op jit(solution)/shard_map/reduce_sum | solution.py:50
  103.7 5.4 %fusion.16 = (f32[1024,256]{1,0:T(8,128)}, bf16[1024,256]{1,0:T(8,128)(2,1)}) fusion(f32[1024,256]{1,0:T(8,128)} %all-reduce.3.cloned.1.call-done, bf16[1024,1024]{1,0:T(8,128)(2,1)} %convolution_convert_fusion, f32[1024,256]{0,1:T(8,128)} %convolution_bitcast_fusion.3, f32[1,1024,256]{1,2,0:T(8,128)} %copy-done.6, f32[1024,256]{0,1:T(8,128)} %copy.30, ...), kind=kOutput, calls=%fused_computation.35 | convolution fusion | flops 542638080 | bytes 8912896 | tf_op jit(solution)/shard_map/dot_general | solution.py:27
  109.1 0.0 all-reduce.5.cloned.1.call-update
  109.1 0.2 all-gather.6.cloned.1.call-start
  109.4 3.9 %fusion.2 = f32[1024,256]{0,1:T(8,128)} fusion(f32[1024,256]{0,1:T(8,128)} %convolution_bitcast_fusion.3, bf16[1024,1024]{1,0:T(8,128)(2,1)S(1)} %copy-done, bf16[1024,256]{1,0:T(8,128)(2,1)} %get-tuple-element.19, f32[1024,256]{0,1:T(8,128)} %copy.30, f32[1024,256]{0,1:T(8,128)S(1)} %copy.32), kind=kOutput, calls=%fused_computation.12 | convolution fusion | flops 540278784 | bytes 6815744 | tf_op jit(solution)/shard_map/dot_general | solution.py:27
  113.3 0.0 all-gather.6.cloned.1.call-update
  113.3 73.9 %all-reduce.5.cloned.1.call-done = f32[1024,256]{1,0:T(8,128)} async-done(((f32[1024,256]{1,0:T(8,128)}), f32[1024,256]{1,0:T(8,128)}) %all-reduce.5.cloned.1.call-update) | async-done | bytes 1048592 | tf_op jit(solution)/shard_map/psum | solution.py:49
  187.2 3.7 %convolution_bitcast_fusion.2 = f32[1024,256]{0,1:T(8,128)} fusion(bf16[1024,1024]{1,0:T(8,128)(2,1)S(1)} %copy-done, f32[1024,256]{1,0:T(8,128)} %get-tuple-element.18, f32[1024,256]{1,0:T(8,128)} %all-reduce.5.cloned.1.call-done), kind=kOutput, calls=%fused_computation.9 | convolution fusion | flops 539230208 | bytes 5242880 | tf_op jit(solution)/shard_map/dot_general | solution.py:27
  190.9 0.0 all-gather.6.cloned.1.call-done
  190.9 6.1 %reshape.11 = f32[4,1024,256]{1,0,2:T(4,128)} reshape(f32[4096,256]{0,1:T(8,128)} %all-gather.6.cloned.1.call-done) | data formatting | bytes 8388608 | tf_op jit(solution)/shard_map/all_gather | solution.py:50
  196.9 5.7 %reduce_sum.29 = f32[1024,256]{0,1:T(8,128)} reduce(f32[4,1024,256]{1,0,2:T(4,128)} %reshape.11, f32[]{:T(128)} %constant.26.clone.1), dimensions={0}, to_apply=%region_4.5 | reduce | flops 786432 | bytes 5242884 | tf_op jit(solution)/shard_map/reduce_sum | solution.py:50
  202.6 0.0 copy-start.2
  202.7 0.0 copy-start.3
  202.7 2.9 %negate_bitcast_fusion = f32[1,1024,256]{1,2,0:T(8,128)} fusion(f32[1024,256]{0,1:T(8,128)} %reduce_sum.29, f32[1024,256]{0,1:T(8,128)S(1)} %copy.32), kind=kLoop, calls=%fused_computation.19 | loop fusion | flops 3145728 | bytes 3145728 | tf_op jit(solution)/shard_map/neg | solution.py:61
  205.6 0.0 copy-done.2
  205.6 0.0 copy-done.3
  205.6 2.7 %fusion.17 = f32[1024,256]{1,0:T(8,128)S(1)} fusion(bf16[1024,1024]{1,0:T(8,128)(2,1)S(1)} %copy-done.2, f32[1024,256]{0,1:T(8,128)S(1)} %copy-done.3, f32[1024,256]{0,1:T(8,128)} %fusion.2, f32[1024,256]{0,1:T(8,128)} %reduce_sum.29, f32[1024,256]{0,1:T(8,128)S(1)} %copy.32), kind=kOutput, calls=%fused_computation.36 | convolution fusion | flops 540540928 | bytes 7340032 | tf_op jit(solution)/shard_map/dot_general | solution.py:27
  208.3 0.0 copy-start.4
  208.3 1.0 copy-done.4
  209.3 1.8 fusion.4
  211.0 0.0 copy-start.1
  211.0 0.0 copy-start.5
  211.0 0.0 copy-start.7
  211.0 2.7 %copy.36 = f32[1,1024,256]{2,1,0:T(8,128)} copy(f32[1,1024,256]{1,2,0:T(8,128)} %fusion.4) | data formatting | bytes 2097152
  213.7 2.5 %copy.37 = f32[1,1024,256]{2,1,0:T(8,128)} copy(f32[1,1024,256]{1,2,0:T(8,128)} %negate_bitcast_fusion) | data formatting | bytes 2097152
  216.2 0.0 copy-done.1
  216.2 0.0 copy-done.5
  216.2 0.0 copy-done.7
  216.2 1.8 subtract_bitcast_fusion.1
Async XLA Ops:
  8.0 2.9 %copy-start.8 = (f32[1,1024,256]{2,1,0:T(8,128)S(1)}, f32[1,1024,256]{2,1,0:T(8,128)}, u32[]{:S(2)}) copy-start(f32[1,1024,256]{2,1,0:T(8,128)} %param.10) | copy-start | bytes 3145732
  8.0 85.9 %all-reduce.3.cloned.1.call-start = ((), (), s32[]{:S(2)}) async-start(), calls=%async_computation | async-start | bytes 2097152 | tf_op jit(solution)/shard_map/psum | solution.py:49
  10.8 1.2 copy-start.9
  10.8 86.8 %all-gather.4.cloned.1.call-start = ((), (), s32[]{:S(2)}) async-start(), calls=%async_computation.1 | async-start | bytes 5242880 | tf_op jit(solution)/shard_map/all_gather | solution.py:50
  12.5 4.0 %copy-start.6 = (f32[1,1024,256]{1,2,0:T(8,128)}, f32[1,1024,256]{1,2,0:T(8,128)S(1)}, u32[]{:S(2)}) copy-start(f32[1,1024,256]{1,2,0:T(8,128)S(1)} %add.45) | copy-start | bytes 3145732
  12.5 2.4 %copy-start = (bf16[1024,1024]{1,0:T(8,128)(2,1)S(1)}, bf16[1024,1024]{1,0:T(8,128)(2,1)}, u32[]{:S(2)}) copy-start(bf16[1024,1024]{1,0:T(8,128)(2,1)} %param.6) | copy-start | bytes 6291460
  13.8 173.4 %all-reduce.5.cloned.1.call-start = ((), (), s32[]{:S(2)}) async-start(), calls=%async_computation.2 | async-start | bytes 2097152 | tf_op jit(solution)/shard_map/psum | solution.py:49
  21.2 2.0 copy-start.10
  109.1 81.7 %all-gather.6.cloned.1.call-start = ((), (), s32[]{:S(2)}) async-start(), calls=%async_computation.3 | async-start | bytes 5242880 | tf_op jit(solution)/shard_map/all_gather | solution.py:50
  202.6 2.9 %copy-start.2 = (bf16[1024,1024]{1,0:T(8,128)(2,1)S(1)}, bf16[1024,1024]{1,0:T(8,128)(2,1)}, u32[]{:S(2)}) copy-start(bf16[1024,1024]{1,0:T(8,128)(2,1)} %convolution_convert_fusion) | copy-start | bytes 6291460
  202.7 2.9 %copy-start.3 = (f32[1024,256]{0,1:T(8,128)S(1)}, f32[1024,256]{0,1:T(8,128)}, u32[]{:S(2)}) copy-start(f32[1024,256]{0,1:T(8,128)} %convolution_bitcast_fusion.2) | copy-start | bytes 3145732
  208.3 1.0 copy-start.4
  211.0 5.2 %copy-start.1 = (f32[1024,256]{1,0:T(8,128)S(1)}, f32[1024,256]{1,0:T(8,128)}, u32[]{:S(2)}) copy-start(f32[1024,256]{1,0:T(8,128)} %get-tuple-element.18) | copy-start | bytes 3145732
  211.0 5.2 %copy-start.5 = (f32[1024,256]{1,0:T(8,128)S(1)}, f32[1024,256]{1,0:T(8,128)}, u32[]{:S(2)}) copy-start(f32[1024,256]{1,0:T(8,128)} %copy-done.4) | copy-start | bytes 3145732
  211.0 5.2 %copy-start.7 = (f32[1024,256]{1,0:T(8,128)S(1)}, f32[1024,256]{1,0:T(8,128)}, u32[]{:S(2)}) copy-start(f32[1024,256]{1,0:T(8,128)} %all-reduce.5.cloned.1.call-done) | copy-start | bytes 3145732
Sparse Core Ops, SparseCore 0:
  12.9 81.0 all-reduce.2
  109.3 77.9 all-reduce.4
Sparse Core Ops, SparseCore 1:
  13.9 37.0 all-gather.3
  113.4 33.9 all-gather.5
